TPU v7x, 768 devices: a whole 4x8x12 slice. The times are simulated.
768 devices in a mesh: dp: 32 (over z_lo, y), seq: 24 (over z_hi, x, core).
Axes of the slice: x: 4, y: 8, z: 12 (z_hi: 3, z_lo: 4; z = z_hi * 4 + z_lo), core: 2. Of those that a mesh axis runs over, the one named last changes fastest.
Arguments:
- queries: bfloat16 [32, 3072, 6144], P('dp', 'seq'), may hold values from -6 to 6
- keys: bfloat16 [32, 3072, 768], P('dp', 'seq'), may hold values from -6 to 6
- values: bfloat16 [32, 3072, 768], P('dp', 'seq'), may hold values from -6 to 6
- segments: int32 [32, 3072], P('dp'), may hold values from 0 to 11, never falling along the last dimension, each value on 1 to 384 neighbouring positions
Outputs:
- attended: bfloat16 [32, 3072, 6144], P('dp', 'seq')
- query_factor: float32 [48], replicated
- key_head_factor: float32 [6], replicated
Inputs may be any that keep to these rules, and one draw needn't show every extreme that they name: `segments`: each row's ids never fall; a document holds at most 384 positions, and some document holds exactly 384.
All inputs are finite; a program needn't handle non-finite values.
Results may differ from a plain program's by a relative error of at most 0.0046.
Values may be sent and summed in bfloat16 or wider, within the bound.
A program may use at most 32 MiB of HBM per device.

v0:
```python
import jax
import jax.numpy as jnp
import numpy as np
from jax import lax
from jax.sharding import PartitionSpec as P

QUERY_HEADS = 48
KEY_VALUE_HEADS = 6
HEAD_SIZE = 128
DOCUMENT_LIMIT = 384


clip_level = 6.0


def attend(query_block, key_block, value_block, query_pos, key_pos, doc_ids):
    scale = query_block.shape[-1] ** (-0.5)
    logits = (
        jnp.einsum("qcgd,kcd->cgqk", query_block, key_block, preferred_element_type=jnp.float32)
        * scale
    )
    query_doc = jnp.take(doc_ids, query_pos)
    key_doc = jnp.take(doc_ids, jnp.maximum(key_pos, 0))
    valid = (
        (key_pos[None, :] <= query_pos[:, None])
        & (key_pos[None, :] >= 0)
        & (key_doc[None, :] == query_doc[:, None])
    )
    logits = jnp.where(valid, logits, -1e30)
    largest = jnp.max(logits, axis=-1, keepdims=True)
    expo = jnp.exp(logits - largest)
    total = jnp.sum(expo, axis=-1, keepdims=True)
    weights = (expo / total).astype(jnp.bfloat16)
    mixed = jnp.einsum(
        "cgqk,kcd->qcgd", weights, value_block, preferred_element_type=jnp.float32
    ).astype(jnp.bfloat16)
    return (mixed, jnp.max(largest[..., 0], axis=-1))


def clip_factors(head_max):
    query_group = QUERY_HEADS // KEY_VALUE_HEADS
    clipped_logits = clip_level / jnp.maximum(head_max, clip_level)
    key_head_factor = jnp.sqrt(
        jnp.min(clipped_logits.reshape(KEY_VALUE_HEADS, query_group), axis=1)
    )
    query_factor = clipped_logits / jnp.repeat(key_head_factor, query_group)
    return (query_factor, key_head_factor)


def local(queries, keys, values, segments):
    query_group = QUERY_HEADS // KEY_VALUE_HEADS
    devices = lax.axis_size("seq")
    rank_index = lax.axis_index("seq")
    rows_per_shard = queries.shape[1]
    total_rows = segments.shape[1]
    doc_ids = segments[0]
    resident_count = QUERY_HEADS // devices
    position_slots = min(
        KEY_VALUE_HEADS,
        (resident_count - 1) // query_group + 1 + min(1, query_group % resident_count),
    )
    block = min(512, total_rows)
    blocks = total_rows // block
    table = np.array(
        [
            min(owning_shard * resident_count // query_group + position_slot, KEY_VALUE_HEADS - 1)
            for owning_shard in range(devices)
            for position_slot in range(position_slots)
        ],
        dtype=np.int32,
    )
    query_cols = lax.all_to_all(queries[0], "seq", split_axis=1, concat_axis=0, tiled=True)
    paired = jnp.stack(
        [
            keys[0].reshape(rows_per_shard, KEY_VALUE_HEADS, HEAD_SIZE),
            values[0].reshape(rows_per_shard, KEY_VALUE_HEADS, HEAD_SIZE),
        ],
        axis=2,
    )
    chosen = jnp.take(paired, jnp.asarray(table), axis=1).reshape(
        rows_per_shard, devices * position_slots * 2 * HEAD_SIZE
    )
    arrived = lax.all_to_all(chosen, "seq", split_axis=1, concat_axis=0, tiled=True).reshape(
        total_rows, position_slots, 2, HEAD_SIZE
    )
    padded = jnp.concatenate(
        [jnp.zeros((DOCUMENT_LIMIT, position_slots, 2, HEAD_SIZE), jnp.bfloat16), arrived], axis=0
    )
    pieces = []
    maxima = []
    for local_head in range(resident_count):
        first_head = rank_index * resident_count
        slot_index = (first_head + local_head) // query_group - first_head // query_group
        head_pairs = lax.dynamic_index_in_dim(padded, slot_index, 1, keepdims=False)
        head_queries = query_cols[:, local_head * HEAD_SIZE : (local_head + 1) * HEAD_SIZE]

        def one_block(number):
            start = number * block
            query_block = lax.dynamic_slice_in_dim(head_queries, start, block, 0)[:, None, None, :]
            window = lax.dynamic_slice_in_dim(head_pairs, start, block + DOCUMENT_LIMIT, 0)
            query_pos = jnp.arange(block, dtype=jnp.int32) + start
            key_pos = jnp.arange(block + DOCUMENT_LIMIT, dtype=jnp.int32) + (start - DOCUMENT_LIMIT)
            mixed, largest = attend(
                query_block,
                window[:, 0][:, None, :],
                window[:, 1][:, None, :],
                query_pos,
                key_pos,
                doc_ids,
            )
            return (mixed[:, 0, 0, :], largest[0, 0])

        outputs, block_max = lax.map(one_block, jnp.arange(blocks, dtype=jnp.int32))
        pieces.append(outputs.reshape(total_rows, HEAD_SIZE))
        maxima.append(jnp.max(block_max))
    head_outputs = jnp.concatenate(pieces, axis=1)
    attended = lax.all_to_all(head_outputs, "seq", split_axis=0, concat_axis=1, tiled=True)
    local_max = jnp.stack(maxima)
    owners = jnp.arange(QUERY_HEADS, dtype=jnp.int32) // resident_count
    candidates = jnp.where(owners == rank_index, jnp.tile(local_max, devices), -1e30)
    head_max = lax.pmax(candidates, ("dp", "seq"))
    query_factor, key_head_factor = clip_factors(head_max)
    return (attended[None], query_factor, key_head_factor)


def solution(mesh):
    in_specs = (P("dp", "seq", None), P("dp", "seq", None), P("dp", "seq", None), P("dp", None))
    out_specs = (P("dp", "seq", None), P(), P())
    return jax.shard_map(local, mesh=mesh, in_specs=in_specs, out_specs=out_specs, check_vma=False)
```

profile of v0, /device:TPU:1, one launch (start us, length us, event | category | flops | bytes accessed | tf_op | source)
XLA Modules:
  0.0 457.1 jit_solution(3483250331577812391)
XLA Ops:
  6.3 18.1 %all-to-all-start = ((bf16[128,24,256]{0,2,1:T(8,128)(2,1)}), bf16[128,24,256]{0,2,1:T(8,128)(2,1)S(1)}, u32[]{:S(2)}, u32[]{:S(2)}) async-start(bf16[128,24,256]{0,2,1:T(8,128)(2,1)} %bitcast.23), calls=%async_computation | async-start | bytes 3145728 | tf_op jit(solution)/shard_map/all_to_all | solution.py:83
  26.3 46.8 %all-to-all-done = bf16[128,24,256]{0,2,1:T(8,128)(2,1)S(1)} async-done(((bf16[128,24,256]{0,2,1:T(8,128)(2,1)}), bf16[128,24,256]{0,2,1:T(8,128)(2,1)S(1)}, u32[]{:S(2)}, u32[]{:S(2)}) %all-to-all-start) | async-done | bytes 1572896 | tf_op jit(solution)/shard_map/all_to_all | solution.py:83
  73.1 9.2 %all-to-all-start.1 = ((bf16[128,24,256]{2,0,1:T(8,128)(2,1)}), bf16[128,24,256]{2,0,1:T(8,128)(2,1)S(1)}, u32[]{:S(2)}, u32[]{:S(2)}) async-start(bf16[128,24,256]{2,0,1:T(8,128)(2,1)} %copy.23), calls=%async_computation.1 | async-start | bytes 3145728 | tf_op jit(solution)/shard_map/all_to_all | solution.py:72
  84.4 3.7 reshape.408
  91.9 35.9 %all-to-all-done.1 = bf16[128,24,256]{2,0,1:T(8,128)(2,1)S(1)} async-done(((bf16[128,24,256]{2,0,1:T(8,128)(2,1)}), bf16[128,24,256]{2,0,1:T(8,128)(2,1)S(1)}, u32[]{:S(2)}, u32[]{:S(2)}) %all-to-all-start.1) | async-done | bytes 1572896 | tf_op jit(solution)/shard_map/all_to_all | solution.py:72
  129.2 90.7 %while.28 = (s32[]{:T(128)}, bf16[6,512,128]{2,1,0:T(8,128)(2,1)S(1)}, f32[6]{0:T(128)S(1)}, s32[6]{0:T(128)S(1)}, bf16[3456,2,128]{2,0,1:T(8,128)(2,1)}, /*inde...) while((s32[]{:T(128)}, ...), condition=%wide.region_4.7_spmd, body=%wide.region_0.6_spmd.sunk | while | flops 240924672 | bytes 6827048 | solution.py:113
  130.5 5.2 %gather_fusion.1 = s32[896]{0:T(1024)S(1)} fusion(s32[3072]{0:T(1024)S(1)} %get-tuple-element.445, s32[1024]{0:T(1024)S(1)} %pad_clamp_fusion.10), kind=kCustom, calls=%fused_computation.clone.clone.1 | custom fusion | bytes 10752 | tf_op jit(solution)/shard_map/while/body/eval_jaxpr/jit(_take)/gather | solution.py:23
  135.7 3.1 gather_fusion
  145.6 5.2 %gather_fusion.1 = s32[896]{0:T(1024)S(1)} fusion(s32[3072]{0:T(1024)S(1)} %get-tuple-element.445, s32[1024]{0:T(1024)S(1)} %pad_clamp_fusion.10), kind=kCustom, calls=%fused_computation.clone.clone.1 | custom fusion | bytes 10752 | tf_op jit(solution)/shard_map/while/body/eval_jaxpr/jit(_take)/gather | solution.py:23
  150.8 3.1 gather_fusion
  160.7 5.2 %gather_fusion.1 = s32[896]{0:T(1024)S(1)} fusion(s32[3072]{0:T(1024)S(1)} %get-tuple-element.445, s32[1024]{0:T(1024)S(1)} %pad_clamp_fusion.10), kind=kCustom, calls=%fused_computation.clone.clone.1 | custom fusion | bytes 10752 | tf_op jit(solution)/shard_map/while/body/eval_jaxpr/jit(_take)/gather | solution.py:23
  165.9 3.1 gather_fusion
  175.8 5.2 %gather_fusion.1 = s32[896]{0:T(1024)S(1)} fusion(s32[3072]{0:T(1024)S(1)} %get-tuple-element.445, s32[1024]{0:T(1024)S(1)} %pad_clamp_fusion.10), kind=kCustom, calls=%fused_computation.clone.clone.1 | custom fusion | bytes 10752 | tf_op jit(solution)/shard_map/while/body/eval_jaxpr/jit(_take)/gather | solution.py:23
  181.0 3.1 gather_fusion
  190.9 5.2 %gather_fusion.1 = s32[896]{0:T(1024)S(1)} fusion(s32[3072]{0:T(1024)S(1)} %get-tuple-element.445, s32[1024]{0:T(1024)S(1)} %pad_clamp_fusion.10), kind=kCustom, calls=%fused_computation.clone.clone.1 | custom fusion | bytes 10752 | tf_op jit(solution)/shard_map/while/body/eval_jaxpr/jit(_take)/gather | solution.py:23
  196.1 3.1 gather_fusion
  206.0 5.2 %gather_fusion.1 = s32[896]{0:T(1024)S(1)} fusion(s32[3072]{0:T(1024)S(1)} %get-tuple-element.445, s32[1024]{0:T(1024)S(1)} %pad_clamp_fusion.10), kind=kCustom, calls=%fused_computation.clone.clone.1 | custom fusion | bytes 10752 | tf_op jit(solution)/shard_map/while/body/eval_jaxpr/jit(_take)/gather | solution.py:23
  211.2 3.1 gather_fusion
  221.6 101.2 %while.29 = (s32[]{:T(128)}, bf16[6,512,128]{2,1,0:T(8,128)(2,1)S(1)}, f32[6]{0:T(128)}, s32[6]{0:T(128)}, bf16[3456,2,128]{2,0,1:T(8,128)(2,1)}, /*index=5*/s32...) while((s32[]{:T(128)}, ...), condition=%wide.region_9.12_spmd, body=%wide.region_5.11_spmd.sunk | while | flops 240924672 | bytes 6827048 | solution.py:113
  223.4 5.2 %gather_fusion.3 = s32[896]{0:T(1024)S(1)} fusion(s32[3072]{0:T(1024)S(1)} %get-tuple-element.403, s32[1024]{0:T(1024)S(1)} %pad_clamp_fusion.12), kind=kCustom, calls=%fused_computation.2.clone.clone.1 | custom fusion | bytes 10752 | tf_op jit(solution)/shard_map/while/body/eval_jaxpr/jit(_take)/gather | solution.py:23
  228.6 3.1 gather_fusion.2
  240.3 5.2 %gather_fusion.3 = s32[896]{0:T(1024)S(1)} fusion(s32[3072]{0:T(1024)S(1)} %get-tuple-element.403, s32[1024]{0:T(1024)S(1)} %pad_clamp_fusion.12), kind=kCustom, calls=%fused_computation.2.clone.clone.1 | custom fusion | bytes 10752 | tf_op jit(solution)/shard_map/while/body/eval_jaxpr/jit(_take)/gather | solution.py:23
  245.5 3.1 gather_fusion.2
  257.2 5.2 %gather_fusion.3 = s32[896]{0:T(1024)S(1)} fusion(s32[3072]{0:T(1024)S(1)} %get-tuple-element.403, s32[1024]{0:T(1024)S(1)} %pad_clamp_fusion.12), kind=kCustom, calls=%fused_computation.2.clone.clone.1 | custom fusion | bytes 10752 | tf_op jit(solution)/shard_map/while/body/eval_jaxpr/jit(_take)/gather | solution.py:23
  262.4 3.1 gather_fusion.2
  274.0 5.2 %gather_fusion.3 = s32[896]{0:T(1024)S(1)} fusion(s32[3072]{0:T(1024)S(1)} %get-tuple-element.403, s32[1024]{0:T(1024)S(1)} %pad_clamp_fusion.12), kind=kCustom, calls=%fused_computation.2.clone.clone.1 | custom fusion | bytes 10752 | tf_op jit(solution)/shard_map/while/body/eval_jaxpr/jit(_take)/gather | solution.py:23
  279.2 3.1 gather_fusion.2
  290.9 5.2 %gather_fusion.3 = s32[896]{0:T(1024)S(1)} fusion(s32[3072]{0:T(1024)S(1)} %get-tuple-element.403, s32[1024]{0:T(1024)S(1)} %pad_clamp_fusion.12), kind=kCustom, calls=%fused_computation.2.clone.clone.1 | custom fusion | bytes 10752 | tf_op jit(solution)/shard_map/while/body/eval_jaxpr/jit(_take)/gather | solution.py:23
  307.7 5.2 %gather_fusion.3 = s32[896]{0:T(1024)S(1)} fusion(s32[3072]{0:T(1024)S(1)} %get-tuple-element.403, s32[1024]{0:T(1024)S(1)} %pad_clamp_fusion.12), kind=kCustom, calls=%fused_computation.2.clone.clone.1 | custom fusion | bytes 10752 | tf_op jit(solution)/shard_map/while/body/eval_jaxpr/jit(_take)/gather | solution.py:23
  312.9 3.1 gather_fusion.2
  324.1 12.6 %all-to-all-start.2 = ((bf16[24,128,256]{2,1,0:T(8,128)(2,1)}), bf16[24,128,256]{2,1,0:T(8,128)(2,1)S(1)}, u32[]{:S(2)}, u32[]{:S(2)}) async-start(bf16[24,128,256]{2,1,0:T(8,128)(2,1)} %pad_maximum_fusion), calls=%async_computation.2 | async-start | bytes 3145728 | tf_op jit(solution)/shard_map/all_to_all | solution.py:117
  339.5 114.3 %pmax.7 = f32[48]{0:T(128)S(1)} all-reduce(f32[48]{0:T(128)S(1)} %compare_select_fusion.4), channel_id=1, replica_groups=mesh['dp'=32,'seq'=24] {'dp','seq'}, use_global_device_ids=true, to_apply=%region_12.15 | all-reduce | flops 48 | bytes 384 | tf_op jit(solution)/shard_map/pmax | solution.py:121
  (218 shorter events, 110.4 us)
Async XLA Ops:
  6.3 18.1 %copy-start.1 = (bf16[1,128,6144]{2,1,0:T(8,128)(2,1)S(1)}, bf16[1,128,6144]{2,1,0:T(8,128)(2,1)}, u32[]{:S(2)}) copy-start(bf16[1,128,6144]{2,1,0:T(8,128)(2,1)} %param.13) | copy-start | bytes 4718596
  6.3 66.8 %all-to-all-start = ((bf16[128,24,256]{0,2,1:T(8,128)(2,1)}), bf16[128,24,256]{0,2,1:T(8,128)(2,1)S(1)}, u32[]{:S(2)}, u32[]{:S(2)}) async-start(bf16[128,24,256]{0,2,1:T(8,128)(2,1)} %bitcast.23), calls=%async_computation | async-start | bytes 3145728 | tf_op jit(solution)/shard_map/all_to_all | solution.py:83
  73.1 54.8 %all-to-all-start.1 = ((bf16[128,24,256]{2,0,1:T(8,128)(2,1)}), bf16[128,24,256]{2,0,1:T(8,128)(2,1)S(1)}, u32[]{:S(2)}, u32[]{:S(2)}) async-start(bf16[128,24,256]{2,0,1:T(8,128)(2,1)} %copy.23), calls=%async_computation.1 | async-start | bytes 3145728 | tf_op jit(solution)/shard_map/all_to_all | solution.py:72
  127.8 1.4 copy-start
  219.9 0.5 copy-start.4
  324.1 12.6 %copy-start.5 = (f32[6]{0:T(128)S(1)}, f32[6]{0:T(128)}, u32[]{:S(2)}) copy-start(f32[6]{0:T(128)} %copy-done.4) | copy-start | bytes 76
  324.1 13.3 %copy-start.3 = (f32[6]{0:T(128)S(1)}, f32[6]{0:T(128)}, u32[]{:S(2)}) copy-start(f32[6]{0:T(128)} %get-tuple-element.188) | copy-start | bytes 76
  324.1 130.6 %all-to-all-start.2 = ((bf16[24,128,256]{2,1,0:T(8,128)(2,1)}), bf16[24,128,256]{2,1,0:T(8,128)(2,1)S(1)}, u32[]{:S(2)}, u32[]{:S(2)}) async-start(bf16[24,128,256]{2,1,0:T(8,128)(2,1)} %pad_maximum_fusion), calls=%async_computation.2 | async-start | bytes 3145728 | tf_op jit(solution)/shard_map/all_to_all | solution.py:117
  454.0 3.2 copy-start.2
where the time goes:
time: 459 us; the launch traced here: 457 us
  local copies, waits for them, and re-layouts  150 us (33%)
  blocking collectives  114 us (25%)
  waiting for transfers between devices  82.7 us (18%)
  matrix products  41.4 us (9%)
  starting transfers between devices  39.8 us (9%)
  other arithmetic  19.4 us (4%)
  loops' own time  8.91 us (2%)
    pmax x1, blocking collectives, local(): head_max = lax.pmax(candidates, ('dp', 'seq'))  114 us
    gather x12, local copies, waits for them, and re-layouts, attend(): key_doc = jnp.take(doc_ids, jnp.maximum(key_pos, 0))  62 us
    all_to_all x1, waiting for transfers between devices, local(): lax.all_to_all(chosen, 'seq', split_axis=1, concat_axis=0, tiled=True)  46.8 us
    gather x12, local copies, waits for them, and re-layouts, attend(): query_doc = jnp.take(doc_ids, query_pos)  37.7 us
    all_to_all x1, waiting for transfers between devices, local(): lax.all_to_all(queries[0], 'seq', split_axis=1, concat_axis=0, tiled=True)  35.9 us
    dot_general x12, matrix products, attend(): jnp.einsum('qcgd,kcd->cgqk', query_block, key_block, preferred_element_ty...  24.3 us
    all_to_all x1, starting transfers between devices, local(): lax.all_to_all(chosen, 'seq', split_axis=1, concat_axis=0, tiled=True)  18.1 us
    dot_general x12, matrix products, attend(): jnp.einsum('cgqk,kcd->qcgd', weights, value_block, preferred_element_type...  17.1 us
  transfers between devices with their start and end apart: 3, of which 2 were waited for; matrix products, arithmetic and copies ran while one was open for 3% of the time, Pallas kernels for 0%

commit v1 on v0

v1 whole, which is shorter than its diff:
```python
import functools
import math

import jax
import jax.numpy as jnp
from jax import lax
from jax.experimental import pallas as pl
from jax.experimental.pallas import tpu as pltpu
from jax.sharding import PartitionSpec as P

QUERY_HEADS = 48
KV_HEADS = 6
GROUP = QUERY_HEADS // KV_HEADS
HEAD = 128
ROWS = 128
CLIP = 6.0
NEG = -1e30
SCALE = HEAD**-0.5
CHUNKS = 2
CROWS = ROWS // CHUNKS
MESH = pl.DeviceIdType.MESH
BF16, F32 = jnp.bfloat16, jnp.float32

F1, F2, F34, F5, CROSS, RELAY, RELAY2 = range(7)
R1, R2, R3, RB = range(4)


def kernel(
    q_hbm, k_hbm, v_hbm, seg_ref, out_hbm, fac_ref,
    q_ref, kall, vall, relay, bias_ref, s_ref, rm_ref, p_ref, o_ref, hm_ref,
    ar_a, ar_b, ar_c,
    load_sem, out_sem, send_sem, recv_sem, a_send, a_recv, b_send, b_recv, c_send, c_recv,
):
    dp, s = lax.axis_index("dp"), lax.axis_index("seq")
    core = lax.rem(s, 2)
    r8 = lax.rem(s, 8)
    zh = lax.div(s, 8)
    x = lax.div(r8, 2)
    y = lax.rem(dp, 8)
    zl = lax.div(dp, 8)
    z = zh * 4 + zl

    def dev_a(k):
        return (dp, zh * 8 + lax.rem(r8 + k, 8))

    def dev_b(k):
        return (zl * 8 + lax.rem(y + k, 8), s)

    def dev_c(k):
        zz = lax.rem(z + k, 12)
        return (lax.rem(zz, 4) * 8 + y, lax.div(zz, 4) * 8 + r8)

    barrier = pltpu.get_barrier_semaphore()
    for n, dev in ((8, dev_a), (8, dev_b), (12, dev_c)):
        for k in range(1, n):
            pl.semaphore_signal(barrier, inc=1, device_id=dev(k), device_id_type=MESH)

    load_k = pltpu.make_async_copy(k_hbm, kall.at[pl.ds(3 * ROWS, ROWS)], load_sem.at[0])
    load_q = pltpu.make_async_copy(q_hbm, q_ref, load_sem.at[1])
    load_v = pltpu.make_async_copy(v_hbm, vall.at[pl.ds(3 * ROWS, ROWS)], load_sem.at[2])
    load_k.start()
    load_q.start()
    load_v.start()

    for d in (1, 2, 3):
        @pl.when(s < d)
        def _():
            zero = jnp.zeros((ROWS, KV_HEADS * HEAD), BF16)
            kall[pl.ds((3 - d) * ROWS, ROWS), :] = zero
            vall[pl.ds((3 - d) * ROWS, ROWS), :] = zero

    def seg_row(block):
        start = pl.multiple_of(jnp.maximum(block, 0) * ROWS, ROWS)
        return seg_ref[:, pl.ds(start, ROWS)].astype(F32)

    own = jnp.broadcast_to(seg_row(s), (ROWS, ROWS))
    query_doc = jnp.transpose(own)
    row = lax.broadcasted_iota(jnp.int32, (ROWS, ROWS), 0)
    col = lax.broadcasted_iota(jnp.int32, (ROWS, ROWS), 1)
    for t in range(4):
        key_doc = jnp.broadcast_to(seg_row(s - 3 + t), (ROWS, ROWS))
        gap = jnp.abs(key_doc - query_doc)
        if t == 3:
            gap = gap + jnp.maximum(col - row, 0).astype(F32)
        else:
            gap = gap + jnp.where(s - 3 + t < 0, 1.0, 0.0)
        bias_ref[t] = jnp.where(gap > 0.5, NEG, 0.0)
    hm_ref[...] = jnp.full((ROWS, ROWS), NEG, F32)

    def s_block(t, last):
        def body(c, carry):
            base = c * (GROUP * HEAD)
            qc = jnp.concatenate(
                [
                    q_ref[:, pl.ds(pl.multiple_of(base + g * HEAD, HEAD), HEAD)]
                    for g in range(GROUP)
                ],
                axis=0,
            )
            kb = kall[pl.ds(t * ROWS, ROWS), pl.ds(pl.multiple_of(c * HEAD, HEAD), HEAD)]
            lg = lax.dot_general(qc, kb, (((1,), (1,)), ((), ())), preferred_element_type=F32)
            lg = lg.reshape(GROUP, ROWS, ROWS) + bias_ref[t][None]
            s_ref[c, t] = lg.reshape(GROUP * ROWS, ROWS)
            mx = lg
            if t != 3:
                mx = jnp.maximum(mx, rm_ref[c].reshape(GROUP, ROWS, ROWS))
            rm_ref[c] = mx.reshape(GROUP * ROWS, ROWS)
            if last:
                hm_ref[pl.ds(pl.multiple_of(c * GROUP, GROUP), GROUP), :] = jnp.max(mx, axis=1)
            return carry

        lax.fori_loop(0, KV_HEADS, body, 0)

    load_k.wait()
    load_q.wait()
    s_block(3, False)
    load_v.wait()
    pl.semaphore_wait(barrier, 25)

    bufs = (kall, vall)

    def part(i, d, h):
        return bufs[i].at[pl.ds((3 - d) * ROWS + h * CROWS, CROWS)]

    def relay_part(i, h):
        return relay.at[i, pl.ds(h * CROWS, CROWS)]

    def copy(src, dst, kind, slot, i, h, target):
        return pltpu.make_async_remote_copy(
            src_ref=src,
            dst_ref=dst,
            send_sem=send_sem.at[kind, i, h],
            recv_sem=recv_sem.at[slot, i, h],
            device_id=(dp, target),
            device_id_type=MESH,
        )

    def await_part(slot, i, h):
        dst = relay_part(i, h) if slot == RB else part(i, slot + 1, h)
        copy(dst, dst, F1, slot, i, h, s).wait_recv()

    odd, even = core == 1, core == 0
    flows = {
        "f1": (even, lambda i, h: copy(part(i, 0, h), part(i, 1, h), F1, R1, i, h, s + 1)),
        "f2": (x <= 2, lambda i, h: copy(part(i, 0, h), part(i, 2, h), F2, R2, i, h, s + 2)),
        "f3": (even & (s >= 2), lambda i, h: copy(part(i, 2, h), part(i, 3, h), F34, R3, i, h, s + 1)),
        "f4": (odd & (s >= 2), lambda i, h: copy(part(i, 2, h), part(i, 1, h), F34, R1, i, h, s - 1)),
        "f5": (
            odd & (x >= 1) & (x <= 2),
            lambda i, h: copy(part(i, 2, h), part(i, 3, h), F5, R3, i, h, s + 1),
        ),
        "cross_z": (
            odd & (x >= 2) & (zh <= 1),
            lambda i, h: copy(part(i, 0, h), relay_part(i, h), CROSS, RB, i, h, s + 8),
        ),
        "cross_x": (
            even & (x == 3) & (zh <= 1),
            lambda i, h: copy(part(i, 0, h), relay_part(i, h), CROSS, RB, i, h, s - 6),
        ),
        "relay_z": (
            even & (x == 0) & (zh <= 1),
            lambda i, h: copy(relay_part(i, h), part(i, 2, h), RELAY, R2, i, h, s + 8),
        ),
        "relay_3": (
            odd & (x == 3) & (zh >= 1),
            lambda i, h: copy(relay_part(i, h), part(i, 2, h), RELAY, R2, i, h, s - 6),
        ),
        "relay_3b": (
            odd & (x == 3) & (zh >= 1),
            lambda i, h: copy(relay_part(i, h), part(i, 3, h), RELAY2, R3, i, h, s - 5),
        ),
        "relay_2": (
            odd & (x == 2) & (zh >= 1),
            lambda i, h: copy(relay_part(i, h), part(i, 3, h), RELAY, R3, i, h, s - 5),
        ),
    }

    def start(name, i, h=None, also=None):
        cond, make = flows[name]
        if also is not None:
            cond = cond & also

        @pl.when(cond)
        def _():
            for j in range(CHUNKS) if h is None else (h,):
                make(i, j).start()

    K, V = 0, 1
    start("cross_z", K)
    start("cross_x", K)
    start("f2", K)
    start("f1", K)
    start("cross_z", V)
    start("cross_x", V)
    start("f2", V, also=x == 0)
    start("f1", V)

    @pl.when(flows["relay_z"][0])
    def _():
        for i in (K, V):
            for h in range(CHUNKS):
                await_part(RB, i, h)
                flows["relay_z"][1](i, h).start()

    def take_two(i):
        for h in range(CHUNKS):
            @pl.when(s >= 2)
            def _():
                await_part(R2, i, h)
            start("f4", i, h)
            start("f3", i, h)
            start("f5", i, h)

    def take(slot, i):
        @pl.when(s >= slot + 1)
        def _():
            for h in range(CHUNKS):
                await_part(slot, i, h)

    def take_relay(i):
        for h in range(CHUNKS):
            @pl.when(odd & (x >= 2) & (zh >= 1))
            def _():
                await_part(RB, i, h)
            start("relay_3", i, h)
            start("relay_3b", i, h)
            start("relay_2", i, h)

    take_two(K)
    start("f2", V, also=x > 0)
    s_block(1, False)
    take(R1, K)
    s_block(2, False)
    take(R3, K)
    s_block(0, True)

    def ar_copies(buf, n, dev, sends, recvs):
        return [
            pltpu.make_async_remote_copy(
                src_ref=buf.at[0],
                dst_ref=buf.at[k],
                send_sem=sends.at[k],
                recv_sem=recvs.at[k],
                device_id=dev(k),
                device_id_type=MESH,
            )
            for k in range(1, n)
        ]

    def ar_finish(buf, copies):
        for c in copies:
            c.wait_recv()
        return jnp.max(buf[...], axis=0)

    stage_a = ar_copies(ar_a, 8, dev_a, a_send, a_recv)
    stage_b = ar_copies(ar_b, 8, dev_b, b_send, b_recv)
    stage_c = ar_copies(ar_c, 12, dev_c, c_send, c_recv)

    ar_a[0] = jnp.max(jnp.transpose(hm_ref[...]), axis=0, keepdims=True) * SCALE
    for c in stage_a:
        c.start()
    take_relay(K)

    def p_body(c, carry):
        m = jnp.max(rm_ref[c], axis=1, keepdims=True)
        for t in range(4):
            p = jnp.exp2((s_ref[c, t] - m) * (SCALE * math.log2(math.e)))
            p_ref[c, :, t * ROWS : (t + 1) * ROWS] = p.astype(BF16)
        return carry

    lax.fori_loop(0, KV_HEADS, p_body, 0)

    def out_copy(c):
        cols = pl.ds(c * GROUP * HEAD, GROUP * HEAD)
        return pltpu.make_async_copy(o_ref.at[:, cols], out_hbm.at[:, cols], out_sem.at[c])

    def finish_values():
        take_two(V)
        take(R1, V)
        take(R3, V)
        for c in range(KV_HEADS):
            vc = jnp.concatenate(
                [vall[:, c * HEAD : (c + 1) * HEAD], jnp.ones((4 * ROWS, HEAD), BF16)], axis=1
            )
            acc = jnp.dot(p_ref[c], vc, preferred_element_type=F32)
            o = (acc[:, :HEAD] / acc[:, HEAD:]).astype(BF16)
            for g in range(GROUP):
                h = c * GROUP + g
                o_ref[:, h * HEAD : (h + 1) * HEAD] = o[g * ROWS : (g + 1) * ROWS]
            out_copy(c).start()

    late = (s >= 8) & (r8 <= 2)

    @pl.when(jnp.logical_not(late))
    def _():
        finish_values()

    ar_b[0] = ar_finish(ar_a, stage_a)
    for c in stage_b:
        c.start()
    take_relay(V)
    ar_c[0] = ar_finish(ar_b, stage_b)
    for c in stage_c:
        c.start()

    @pl.when(late)
    def _():
        finish_values()

    head_max = ar_finish(ar_c, stage_c)
    clipped = CLIP / jnp.maximum(head_max, CLIP)
    spread = jnp.broadcast_to(clipped, (ROWS, ROWS))
    down = jnp.transpose(spread)
    group = lax.div(row, GROUP)
    big = jnp.full((ROWS, ROWS), jnp.inf, F32)
    per_query = jnp.min(jnp.where(group == lax.div(col, GROUP), down, big), axis=0, keepdims=True)
    per_key = jnp.min(
        jnp.where(group == jnp.minimum(col, KV_HEADS - 1), down, big), axis=0, keepdims=True
    )
    fac_ref[0:1, :] = clipped / jnp.sqrt(per_query)
    fac_ref[1:2, :] = jnp.sqrt(per_key)

    for copies in (stage_a, stage_b, stage_c):
        for c in copies:
            c.wait_send()
    for cond, make in flows.values():
        @pl.when(cond)
        def _():
            for i in (K, V):
                for h in range(CHUNKS):
                    make(i, h).wait_send()
    for c in range(KV_HEADS):
        out_copy(c).wait()


def local(queries, keys, values, segments):
    width, kv_width = QUERY_HEADS * HEAD, KV_HEADS * HEAD
    any_spec = pl.BlockSpec(memory_space=pl.ANY)
    vmem_spec = pl.BlockSpec(memory_space=pltpu.VMEM)
    dma = pltpu.SemaphoreType.DMA
    attended, factors = pl.pallas_call(
        kernel,
        name="packed_attention",
        out_shape=(
            jax.ShapeDtypeStruct((ROWS, width), BF16),
            jax.ShapeDtypeStruct((2, ROWS), F32),
        ),
        in_specs=[any_spec, any_spec, any_spec, vmem_spec],
        out_specs=(any_spec, vmem_spec),
        scratch_shapes=[
            pltpu.VMEM((ROWS, width), BF16),
            pltpu.VMEM((4 * ROWS, kv_width), BF16),
            pltpu.VMEM((4 * ROWS, kv_width), BF16),
            pltpu.VMEM((2, ROWS, kv_width), BF16),
            pltpu.VMEM((4, ROWS, ROWS), F32),
            pltpu.VMEM((KV_HEADS, 4, GROUP * ROWS, ROWS), F32),
            pltpu.VMEM((KV_HEADS, GROUP * ROWS, ROWS), F32),
            pltpu.VMEM((KV_HEADS, GROUP * ROWS, 4 * ROWS), BF16),
            pltpu.VMEM((ROWS, width), BF16),
            pltpu.VMEM((ROWS, ROWS), F32),
            pltpu.VMEM((8, 1, ROWS), F32),
            pltpu.VMEM((8, 1, ROWS), F32),
            pltpu.VMEM((12, 1, ROWS), F32),
            dma((3,)),
            dma((KV_HEADS,)),
            dma((7, 2, CHUNKS)),
            dma((4, 2, CHUNKS)),
            dma((8,)),
            dma((8,)),
            dma((8,)),
            dma((8,)),
            dma((12,)),
            dma((12,)),
        ],
        compiler_params=pltpu.CompilerParams(
            collective_id=0, has_side_effects=True, vmem_limit_bytes=48 * 1024 * 1024
        ),
    )(queries[0], keys[0], values[0], segments)
    return attended[None], factors[0, :QUERY_HEADS], factors[1, :KV_HEADS]


def solution(mesh):
    in_specs = (P("dp", "seq", None), P("dp", "seq", None), P("dp", "seq", None), P("dp", None))
    out_specs = (P("dp", "seq", None), P(), P())
    return jax.shard_map(local, mesh=mesh, in_specs=in_specs, out_specs=out_specs, check_vma=False)
```

time: 459 us -> 74.2 us (0.16)
  the two profiles are of different devices: /device:TPU:1 before, /device:TPU:3 now
where the time goes in v1:
time: 74.2 us; the launch traced here: 74 us
  Pallas kernels  67.2 us (91%)
  local copies, waits for them, and re-layouts  6.13 us (8%)
    pallas_call x1, Pallas kernels, local(): pl.pallas_call(kernel, name='packed_attention', out_shape=(jax.ShapeDtype...  67.2 us
    unnamed x9, local copies, waits for them, and re-layouts  5.1 us

profile of v1, /device:TPU:3, one launch (start us, length us, event | category | flops | bytes accessed | tf_op | source)
XLA Modules:
  0.0 74.0 jit_solution(10735057457205875896)
XLA Ops:
  0.6 0.0 copy-start
  0.6 1.4 %copy-done = bf16[1,128,6144]{2,1,0:T(8,128)(2,1)S(1)} copy-done((bf16[1,128,6144]{2,1,0:T(8,128)(2,1)S(1)}, bf16[1,128,6144]{2,1,0:T(8,128)(2,1)}, u32[]{:S(2)}) %copy-start) | copy-done | bytes 1572888
  2.0 0.0 copy-start.1
  2.0 0.9 %copy-done.1 = bf16[1,128,768]{2,1,0:T(8,128)(2,1)S(1)} copy-done((bf16[1,128,768]{2,1,0:T(8,128)(2,1)S(1)}, bf16[1,128,768]{2,1,0:T(8,128)(2,1)}, u32[]{:S(2)}) %copy-start.1) | copy-done | bytes 196632
  3.0 0.0 copy-start.2
  3.0 0.9 %copy-done.2 = bf16[1,128,768]{2,1,0:T(8,128)(2,1)S(1)} copy-done((bf16[1,128,768]{2,1,0:T(8,128)(2,1)S(1)}, bf16[1,128,768]{2,1,0:T(8,128)(2,1)}, u32[]{:S(2)}) %copy-start.2) | copy-done | bytes 196632
  3.9 0.0 copy-start.3
  3.9 0.7 copy-done.3
  4.6 67.2 %packed_attention.1 = (bf16[128,6144]{1,0:T(8,128)(2,1)S(1)}, f32[2,128]{1,0:T(2,128)S(1)}) custom-call(bf16[128,6144]{1,0:T(8,128)(2,1)S(1)} %bitcast.9, bf16[128,768]{1,0:T(8,128)(2,1)S(1)} %bitcast.10, bf16[128,768]{1,0:T(8,128)(2,1)S(1)} %bitcast.11, s32[1,3072]{1,0:T(1,128)S(1)} %copy-done.3), custom_call_target="tpu_custom_call" | custom-call | tf_op jit(solution)/shard_map/packed_attention/pallas_call | solution.py:341
  71.8 0.5 slice_bitcast_fusion
  72.3 0.5 slice_bitcast_fusion.1
  72.8 1.1 %copy.8 = bf16[1,128,6144]{2,1,0:T(8,128)(2,1)} copy(bf16[1,128,6144]{2,1,0:T(8,128)(2,1)S(1)} %bitcast.8) | data formatting | bytes 3145728
Async XLA Ops:
  0.6 1.4 %copy-start = (bf16[1,128,6144]{2,1,0:T(8,128)(2,1)S(1)}, bf16[1,128,6144]{2,1,0:T(8,128)(2,1)}, u32[]{:S(2)}) copy-start(bf16[1,128,6144]{2,1,0:T(8,128)(2,1)} %param.4) | copy-start | bytes 4718596
  2.0 0.9 %copy-start.1 = (bf16[1,128,768]{2,1,0:T(8,128)(2,1)S(1)}, bf16[1,128,768]{2,1,0:T(8,128)(2,1)}, u32[]{:S(2)}) copy-start(bf16[1,128,768]{2,1,0:T(8,128)(2,1)} %param.5) | copy-start | bytes 589828
  3.0 0.9 %copy-start.2 = (bf16[1,128,768]{2,1,0:T(8,128)(2,1)S(1)}, bf16[1,128,768]{2,1,0:T(8,128)(2,1)}, u32[]{:S(2)}) copy-start(bf16[1,128,768]{2,1,0:T(8,128)(2,1)} %param.6) | copy-start | bytes 589828
  3.9 0.7 copy-start.3

commit v2 on v1

--- a/solution.py
+++ b/solution.py
@@ -21,15 +21,15 @@
 MESH = pl.DeviceIdType.MESH
 BF16, F32 = jnp.bfloat16, jnp.float32
 
-F1, F2, F34, F5, CROSS, RELAY, RELAY2 = range(7)
+F1, F2, F34, F5, CROSS, RELAY = range(6)
 R1, R2, R3, RB = range(4)
 
 
 def kernel(
-    q_hbm, k_hbm, v_hbm, seg_ref, out_hbm, fac_ref,
-    q_ref, kall, vall, relay, bias_ref, s_ref, rm_ref, p_ref, o_ref, hm_ref,
+    q_hbm, k_hbm, v_hbm, seg_hbm, o_ref, fac_ref,
+    q_ref, kall, vall, relay, bias_ref, s_ref, rm_ref, p_ref, seg_ref, hm_ref,
     ar_a, ar_b, ar_c,
-    load_sem, out_sem, send_sem, recv_sem, a_send, a_recv, b_send, b_recv, c_send, c_recv,
+    load_sem, send_sem, recv_sem, a_send, a_recv, b_send, b_recv, c_send, c_recv,
 ):
     dp, s = lax.axis_index("dp"), lax.axis_index("seq")
     core = lax.rem(s, 2)
@@ -50,10 +50,17 @@
         zz = lax.rem(z + k, 12)
         return (lax.rem(zz, 4) * 8 + y, lax.div(zz, 4) * 8 + r8)
 
+    load_seg = pltpu.make_async_copy(seg_hbm, seg_ref, load_sem.at[3])
+    load_seg.start()
     barrier = pltpu.get_barrier_semaphore()
     for n, dev in ((8, dev_a), (8, dev_b), (12, dev_c)):
         for k in range(1, n):
             pl.semaphore_signal(barrier, inc=1, device_id=dev(k), device_id_type=MESH)
+
+    @pl.when((x == 0) & (zh >= 1))
+    def _():
+        source = (dp, s - jnp.where(core == 0, 3, 2))
+        pl.semaphore_signal(barrier, inc=1, device_id=source, device_id_type=MESH)
 
     load_k = pltpu.make_async_copy(k_hbm, kall.at[pl.ds(3 * ROWS, ROWS)], load_sem.at[0])
     load_q = pltpu.make_async_copy(q_hbm, q_ref, load_sem.at[1])
@@ -68,6 +75,8 @@
             zero = jnp.zeros((ROWS, KV_HEADS * HEAD), BF16)
             kall[pl.ds((3 - d) * ROWS, ROWS), :] = zero
             vall[pl.ds((3 - d) * ROWS, ROWS), :] = zero
+
+    load_seg.wait()
 
     def seg_row(block):
         start = pl.multiple_of(jnp.maximum(block, 0) * ROWS, ROWS)
@@ -87,7 +96,7 @@
         bias_ref[t] = jnp.where(gap > 0.5, NEG, 0.0)
     hm_ref[...] = jnp.full((ROWS, ROWS), NEG, F32)
 
-    def s_block(t, last):
+    def s_blocks(first, count, last):
         def body(c, carry):
             base = c * (GROUP * HEAD)
             qc = jnp.concatenate(
@@ -97,13 +106,16 @@
                 ],
                 axis=0,
             )
-            kb = kall[pl.ds(t * ROWS, ROWS), pl.ds(pl.multiple_of(c * HEAD, HEAD), HEAD)]
+            cols = pl.ds(pl.multiple_of(c * HEAD, HEAD), HEAD)
+            kb = kall[pl.ds(first * ROWS, count * ROWS), cols]
             lg = lax.dot_general(qc, kb, (((1,), (1,)), ((), ())), preferred_element_type=F32)
-            lg = lg.reshape(GROUP, ROWS, ROWS) + bias_ref[t][None]
-            s_ref[c, t] = lg.reshape(GROUP * ROWS, ROWS)
-            mx = lg
-            if t != 3:
-                mx = jnp.maximum(mx, rm_ref[c].reshape(GROUP, ROWS, ROWS))
+            mx = None if first == 3 else rm_ref[c].reshape(GROUP, ROWS, ROWS)
+            for n in range(count):
+                t = first + n
+                one = lg[:, n * ROWS : (n + 1) * ROWS].reshape(GROUP, ROWS, ROWS)
+                one = one + bias_ref[t][None]
+                s_ref[c, t] = one.reshape(GROUP * ROWS, ROWS)
+                mx = one if mx is None else jnp.maximum(mx, one)
             rm_ref[c] = mx.reshape(GROUP * ROWS, ROWS)
             if last:
                 hm_ref[pl.ds(pl.multiple_of(c * GROUP, GROUP), GROUP), :] = jnp.max(mx, axis=1)
@@ -113,9 +125,10 @@
 
     load_k.wait()
     load_q.wait()
-    s_block(3, False)
+    s_blocks(3, 1, False)
     load_v.wait()
-    pl.semaphore_wait(barrier, 25)
+    direct = (core == 1) & (x >= 2) & (zh <= 1)
+    pl.semaphore_wait(barrier, 25 + jnp.where(direct, 1, 0))
 
     bufs = (kall, vall)
 
@@ -146,32 +159,24 @@
         "f3": (even & (s >= 2), lambda i, h: copy(part(i, 2, h), part(i, 3, h), F34, R3, i, h, s + 1)),
         "f4": (odd & (s >= 2), lambda i, h: copy(part(i, 2, h), part(i, 1, h), F34, R1, i, h, s - 1)),
         "f5": (
-            odd & (x >= 1) & (x <= 2),
+            odd & (s >= 3) & (x <= 2),
             lambda i, h: copy(part(i, 2, h), part(i, 3, h), F5, R3, i, h, s + 1),
         ),
-        "cross_z": (
-            odd & (x >= 2) & (zh <= 1),
-            lambda i, h: copy(part(i, 0, h), relay_part(i, h), CROSS, RB, i, h, s + 8),
-        ),
-        "cross_x": (
+        "cross_7": (
+            odd & (x == 3) & (zh <= 1),
+            lambda i, h: copy(part(i, 0, h), part(i, 2, h), CROSS, R2, i, h, s + 2),
+        ),
+        "cross_5": (
+            odd & (x == 2) & (zh <= 1),
+            lambda i, h: copy(part(i, 0, h), part(i, 3, h), CROSS, R3, i, h, s + 3),
+        ),
+        "cross_6": (
             even & (x == 3) & (zh <= 1),
             lambda i, h: copy(part(i, 0, h), relay_part(i, h), CROSS, RB, i, h, s - 6),
         ),
-        "relay_z": (
+        "relay_6": (
             even & (x == 0) & (zh <= 1),
             lambda i, h: copy(relay_part(i, h), part(i, 2, h), RELAY, R2, i, h, s + 8),
-        ),
-        "relay_3": (
-            odd & (x == 3) & (zh >= 1),
-            lambda i, h: copy(relay_part(i, h), part(i, 2, h), RELAY, R2, i, h, s - 6),
-        ),
-        "relay_3b": (
-            odd & (x == 3) & (zh >= 1),
-            lambda i, h: copy(relay_part(i, h), part(i, 3, h), RELAY2, R3, i, h, s - 5),
-        ),
-        "relay_2": (
-            odd & (x == 2) & (zh >= 1),
-            lambda i, h: copy(relay_part(i, h), part(i, 3, h), RELAY, R3, i, h, s - 5),
         ),
     }
 
@@ -186,21 +191,26 @@
                 make(i, j).start()
 
     K, V = 0, 1
-    start("cross_z", K)
-    start("cross_x", K)
+
+    def cross(i):
+        start("cross_7", i)
+        start("cross_5", i)
+        start("cross_6", i)
+
+    def take_relay(i, also):
+        for h in range(CHUNKS):
+            @pl.when(flows["relay_6"][0] & also)
+            def _():
+                await_part(RB, i, h)
+                flows["relay_6"][1](i, h).start()
+
+    cross(K)
     start("f2", K)
     start("f1", K)
-    start("cross_z", V)
-    start("cross_x", V)
     start("f2", V, also=x == 0)
-    start("f1", V)
-
-    @pl.when(flows["relay_z"][0])
-    def _():
-        for i in (K, V):
-            for h in range(CHUNKS):
-                await_part(RB, i, h)
-                flows["relay_z"][1](i, h).start()
+    start("f1", V, also=x == 0)
+    take_relay(K, zh >= 0)
+    take_relay(V, zh >= 1)
 
     def take_two(i):
         for h in range(CHUNKS):
@@ -217,22 +227,14 @@
             for h in range(CHUNKS):
                 await_part(slot, i, h)
 
-    def take_relay(i):
-        for h in range(CHUNKS):
-            @pl.when(odd & (x >= 2) & (zh >= 1))
-            def _():
-                await_part(RB, i, h)
-            start("relay_3", i, h)
-            start("relay_3b", i, h)
-            start("relay_2", i, h)
-
     take_two(K)
     start("f2", V, also=x > 0)
-    s_block(1, False)
+    start("f1", V, also=x > 0)
     take(R1, K)
-    s_block(2, False)
+    s_blocks(1, 2, False)
+    cross(V)
     take(R3, K)
-    s_block(0, True)
+    s_blocks(0, 1, True)
 
     def ar_copies(buf, n, dev, sends, recvs):
         return [
@@ -259,7 +261,7 @@
     ar_a[0] = jnp.max(jnp.transpose(hm_ref[...]), axis=0, keepdims=True) * SCALE
     for c in stage_a:
         c.start()
-    take_relay(K)
+    take_relay(V, zh < 1)
 
     def p_body(c, carry):
         m = jnp.max(rm_ref[c], axis=1, keepdims=True)
@@ -270,12 +272,7 @@
 
     lax.fori_loop(0, KV_HEADS, p_body, 0)
 
-    def out_copy(c):
-        cols = pl.ds(c * GROUP * HEAD, GROUP * HEAD)
-        return pltpu.make_async_copy(o_ref.at[:, cols], out_hbm.at[:, cols], out_sem.at[c])
-
     def finish_values():
-        take_two(V)
         take(R1, V)
         take(R3, V)
         for c in range(KV_HEADS):
@@ -287,18 +284,22 @@
             for g in range(GROUP):
                 h = c * GROUP + g
                 o_ref[:, h * HEAD : (h + 1) * HEAD] = o[g * ROWS : (g + 1) * ROWS]
-            out_copy(c).start()
 
     late = (s >= 8) & (r8 <= 2)
 
     @pl.when(jnp.logical_not(late))
     def _():
+        take_two(V)
         finish_values()
 
     ar_b[0] = ar_finish(ar_a, stage_a)
     for c in stage_b:
         c.start()
-    take_relay(V)
+
+    @pl.when(late)
+    def _():
+        take_two(V)
+
     ar_c[0] = ar_finish(ar_b, stage_b)
     for c in stage_c:
         c.start()
@@ -329,13 +330,11 @@
             for i in (K, V):
                 for h in range(CHUNKS):
                     make(i, h).wait_send()
-    for c in range(KV_HEADS):
-        out_copy(c).wait()
 
 
 def local(queries, keys, values, segments):
     width, kv_width = QUERY_HEADS * HEAD, KV_HEADS * HEAD
-    any_spec = pl.BlockSpec(memory_space=pl.ANY)
+    hbm_spec = pl.BlockSpec(memory_space=pltpu.HBM)
     vmem_spec = pl.BlockSpec(memory_space=pltpu.VMEM)
     dma = pltpu.SemaphoreType.DMA
     attended, factors = pl.pallas_call(
@@ -345,8 +344,8 @@
             jax.ShapeDtypeStruct((ROWS, width), BF16),
             jax.ShapeDtypeStruct((2, ROWS), F32),
         ),
-        in_specs=[any_spec, any_spec, any_spec, vmem_spec],
-        out_specs=(any_spec, vmem_spec),
+        in_specs=[hbm_spec, hbm_spec, hbm_spec, hbm_spec],
+        out_specs=(vmem_spec, vmem_spec),
         scratch_shapes=[
             pltpu.VMEM((ROWS, width), BF16),
             pltpu.VMEM((4 * ROWS, kv_width), BF16),
@@ -356,14 +355,13 @@
             pltpu.VMEM((KV_HEADS, 4, GROUP * ROWS, ROWS), F32),
             pltpu.VMEM((KV_HEADS, GROUP * ROWS, ROWS), F32),
             pltpu.VMEM((KV_HEADS, GROUP * ROWS, 4 * ROWS), BF16),
-            pltpu.VMEM((ROWS, width), BF16),
+            pltpu.VMEM(segments.shape, jnp.int32),
             pltpu.VMEM((ROWS, ROWS), F32),
             pltpu.VMEM((8, 1, ROWS), F32),
             pltpu.VMEM((8, 1, ROWS), F32),
             pltpu.VMEM((12, 1, ROWS), F32),
-            dma((3,)),
-            dma((KV_HEADS,)),
-            dma((7, 2, CHUNKS)),
+            dma((4,)),
+            dma((6, 2, CHUNKS)),
             dma((4, 2, CHUNKS)),
             dma((8,)),
             dma((8,)),
@@ -375,7 +373,7 @@
         compiler_params=pltpu.CompilerParams(
             collective_id=0, has_side_effects=True, vmem_limit_bytes=48 * 1024 * 1024
         ),
-    )(queries[0], keys[0], values[0], segments)
+    )(*(pltpu.with_memory_space_constraint(a, pltpu.HBM) for a in (queries[0], keys[0], values[0], segments)))
     return attended[None], factors[0, :QUERY_HEADS], factors[1, :KV_HEADS]
 
 

time: 74.2 us -> 62.8 us (0.85)
  Pallas kernels: 67.2 us -> 59.8 us
  local copies, waits for them, and re-layouts: 6.13 us -> 2.17 us
    pallas_call x1, Pallas kernels: 67.2 us -> 59.8 us  [local(): pl.pallas_call(kernel, name='packed_attention', out_shape=(jax.ShapeDtype...]
    unnamed x9 -> x1, local copies, waits for them, and re-layouts: 5.1 us -> 1.14 us
where the time goes in v2:
time: 62.8 us; the launch traced here: 62.6 us
  Pallas kernels  59.8 us (95%)
  local copies, waits for them, and re-layouts  2.17 us (3%)
  between operations  0.64 us (1%)
    pallas_call x1, Pallas kernels, local(): pl.pallas_call(kernel, name='packed_attention', out_shape=(jax.ShapeDtype...  59.8 us

profile of v2, /device:TPU:3, one launch (start us, length us, event | category | flops | bytes accessed | tf_op | source)
XLA Modules:
  0.0 62.6 jit_solution(13263411009435294680)
XLA Ops:
  0.6 59.8 %packed_attention.1 = (bf16[128,6144]{1,0:T(8,128)(2,1)S(1)}, f32[2,128]{1,0:T(2,128)S(1)}) custom-call(bf16[128,6144]{1,0:T(8,128)(2,1)} %bitcast.9, bf16[128,768]{1,0:T(8,128)(2,1)} %bitcast.10, bf16[128,768]{1,0:T(8,128)(2,1)} %bitcast.11, s32[1,3072]{1,0:T(1,128)} %seg_hbm.1), custom_call_target="tpu_custom_call" | custom-call | tf_op jit(solution)/shard_map/packed_attention/pallas_call | solution.py:340
  60.4 0.5 slice_bitcast_fusion
  60.9 0.5 slice_bitcast_fusion.1
  61.5 1.1 %copy.8 = bf16[1,128,6144]{2,1,0:T(8,128)(2,1)} copy(bf16[1,128,6144]{2,1,0:T(8,128)(2,1)S(1)} %bitcast.8) | data formatting | bytes 3145728

commit v3 on v2

--- a/solution.py
+++ b/solution.py
@@ -16,7 +16,7 @@
 CLIP = 6.0
 NEG = -1e30
 SCALE = HEAD**-0.5
-CHUNKS = 2
+CHUNKS = 4
 CROWS = ROWS // CHUNKS
 MESH = pl.DeviceIdType.MESH
 BF16, F32 = jnp.bfloat16, jnp.float32
@@ -26,8 +26,8 @@
 
 
 def kernel(
-    q_hbm, k_hbm, v_hbm, seg_hbm, o_ref, fac_ref,
-    q_ref, kall, vall, relay, bias_ref, s_ref, rm_ref, p_ref, seg_ref, hm_ref,
+    q_hbm, k_hbm, v_hbm, seg_hbm, o_ref, hmax_ref,
+    q_ref, kall, vall, relay, bias_ref, rm_ref, p_ref, seg_ref, hm_ref,
     ar_a, ar_b, ar_c,
     load_sem, send_sem, recv_sem, a_send, a_recv, b_send, b_recv, c_send, c_recv,
 ):
@@ -59,8 +59,8 @@
 
     @pl.when((x == 0) & (zh >= 1))
     def _():
-        source = (dp, s - jnp.where(core == 0, 3, 2))
-        pl.semaphore_signal(barrier, inc=1, device_id=source, device_id_type=MESH)
+        for back in (jnp.where(core == 0, 3, 2), 6):
+            pl.semaphore_signal(barrier, inc=1, device_id=(dp, s - back), device_id_type=MESH)
 
     load_k = pltpu.make_async_copy(k_hbm, kall.at[pl.ds(3 * ROWS, ROWS)], load_sem.at[0])
     load_q = pltpu.make_async_copy(q_hbm, q_ref, load_sem.at[1])
@@ -96,25 +96,31 @@
         bias_ref[t] = jnp.where(gap > 0.5, NEG, 0.0)
     hm_ref[...] = jnp.full((ROWS, ROWS), NEG, F32)
 
+    def queries_of(c):
+        base = c * (GROUP * HEAD)
+        return jnp.concatenate(
+            [
+                q_ref[:, pl.ds(pl.multiple_of(base + g * HEAD, HEAD), HEAD)]
+                for g in range(GROUP)
+            ],
+            axis=0,
+        )
+
+    def products(c, first, count):
+        cols = pl.ds(pl.multiple_of(c * HEAD, HEAD), HEAD)
+        kb = kall[pl.ds(first * ROWS, count * ROWS), cols]
+        return lax.dot_general(
+            queries_of(c), kb, (((1,), (1,)), ((), ())), preferred_element_type=F32
+        )
+
     def s_blocks(first, count, last):
         def body(c, carry):
-            base = c * (GROUP * HEAD)
-            qc = jnp.concatenate(
-                [
-                    q_ref[:, pl.ds(pl.multiple_of(base + g * HEAD, HEAD), HEAD)]
-                    for g in range(GROUP)
-                ],
-                axis=0,
-            )
-            cols = pl.ds(pl.multiple_of(c * HEAD, HEAD), HEAD)
-            kb = kall[pl.ds(first * ROWS, count * ROWS), cols]
-            lg = lax.dot_general(qc, kb, (((1,), (1,)), ((), ())), preferred_element_type=F32)
+            lg = products(c, first, count)
             mx = None if first == 3 else rm_ref[c].reshape(GROUP, ROWS, ROWS)
             for n in range(count):
                 t = first + n
                 one = lg[:, n * ROWS : (n + 1) * ROWS].reshape(GROUP, ROWS, ROWS)
                 one = one + bias_ref[t][None]
-                s_ref[c, t] = one.reshape(GROUP * ROWS, ROWS)
                 mx = one if mx is None else jnp.maximum(mx, one)
             rm_ref[c] = mx.reshape(GROUP * ROWS, ROWS)
             if last:
@@ -127,7 +133,7 @@
     load_q.wait()
     s_blocks(3, 1, False)
     load_v.wait()
-    direct = (core == 1) & (x >= 2) & (zh <= 1)
+    direct = (((core == 1) & (x >= 2)) | (x == 1)) & (zh <= 1)
     pl.semaphore_wait(barrier, 25 + jnp.where(direct, 1, 0))
 
     bufs = (kall, vall)
@@ -174,11 +180,22 @@
             even & (x == 3) & (zh <= 1),
             lambda i, h: copy(part(i, 0, h), relay_part(i, h), CROSS, RB, i, h, s - 6),
         ),
+        "side": (
+            (x == 3) & (zh <= 1),
+            lambda i, h: copy(part(i, 0, h), relay_part(i, h), CROSS, RB, i, h, s - 4),
+        ),
         "relay_6": (
             even & (x == 0) & (zh <= 1),
             lambda i, h: copy(relay_part(i, h), part(i, 2, h), RELAY, R2, i, h, s + 8),
         ),
+        "relay_1": (
+            (x == 1) & (zh <= 1),
+            lambda i, h: copy(relay_part(i, h), part(i, 2, h), RELAY, R2, i, h, s + 6),
+        ),
     }
+    every = tuple(range(CHUNKS))
+    most, last = every[:-1], every[-1:]
+    chunks_of = {"cross_7": most, "cross_6": most, "relay_6": most, "side": last, "relay_1": last}
 
     def start(name, i, h=None, also=None):
         cond, make = flows[name]
@@ -187,30 +204,32 @@
 
         @pl.when(cond)
         def _():
-            for j in range(CHUNKS) if h is None else (h,):
+            for j in chunks_of.get(name, every) if h is None else (h,):
                 make(i, j).start()
 
     K, V = 0, 1
 
     def cross(i):
+        start("side", i)
         start("cross_7", i)
         start("cross_5", i)
         start("cross_6", i)
 
-    def take_relay(i, also):
-        for h in range(CHUNKS):
-            @pl.when(flows["relay_6"][0] & also)
-            def _():
-                await_part(RB, i, h)
-                flows["relay_6"][1](i, h).start()
+    def take_relay(i):
+        for name in ("relay_6", "relay_1"):
+            cond, make = flows[name]
+            for h in chunks_of[name]:
+                @pl.when(cond)
+                def _():
+                    await_part(RB, i, h)
+                    make(i, h).start()
 
     cross(K)
     start("f2", K)
     start("f1", K)
     start("f2", V, also=x == 0)
     start("f1", V, also=x == 0)
-    take_relay(K, zh >= 0)
-    take_relay(V, zh >= 1)
+    take_relay(K)
 
     def take_two(i):
         for h in range(CHUNKS):
@@ -232,9 +251,9 @@
     start("f1", V, also=x > 0)
     take(R1, K)
     s_blocks(1, 2, False)
-    cross(V)
     take(R3, K)
     s_blocks(0, 1, True)
+    cross(V)
 
     def ar_copies(buf, n, dev, sends, recvs):
         return [
@@ -261,13 +280,17 @@
     ar_a[0] = jnp.max(jnp.transpose(hm_ref[...]), axis=0, keepdims=True) * SCALE
     for c in stage_a:
         c.start()
-    take_relay(V, zh < 1)
+    take_relay(V)
 
     def p_body(c, carry):
-        m = jnp.max(rm_ref[c], axis=1, keepdims=True)
-        for t in range(4):
-            p = jnp.exp2((s_ref[c, t] - m) * (SCALE * math.log2(math.e)))
-            p_ref[c, :, t * ROWS : (t + 1) * ROWS] = p.astype(BF16)
+        m = jnp.max(rm_ref[c], axis=1, keepdims=True).reshape(GROUP, ROWS, 1)
+        for first in (0, 2):
+            lg = products(c, first, 2)
+            for n in range(2):
+                t = first + n
+                one = lg[:, n * ROWS : (n + 1) * ROWS].reshape(GROUP, ROWS, ROWS)
+                p = jnp.exp2(((one + bias_ref[t][None]) - m) * (SCALE * math.log2(math.e)))
+                p_ref[c, :, t * ROWS : (t + 1) * ROWS] = p.astype(BF16).reshape(GROUP * ROWS, ROWS)
         return carry
 
     lax.fori_loop(0, KV_HEADS, p_body, 0)
@@ -309,27 +332,39 @@
         finish_values()
 
     head_max = ar_finish(ar_c, stage_c)
-    clipped = CLIP / jnp.maximum(head_max, CLIP)
-    spread = jnp.broadcast_to(clipped, (ROWS, ROWS))
-    down = jnp.transpose(spread)
-    group = lax.div(row, GROUP)
+    hmax_ref[...] = head_max
+
+    for copies in (stage_a, stage_b, stage_c):
+        for c in copies:
+            c.wait_send()
+    for name, (cond, make) in flows.items():
+        @pl.when(cond)
+        def _():
+            for i in (K, V):
+                for h in chunks_of.get(name, every):
+                    make(i, h).wait_send()
+
+
+def finish(o_ref, hmax_ref, out_hbm, query_ref, key_ref, sem):
+    parts = 4
+    copies = []
+    for n in range(parts):
+        rows = pl.ds(n * (ROWS // parts), ROWS // parts)
+        copies.append(pltpu.make_async_copy(o_ref.at[rows], out_hbm.at[rows], sem.at[n]))
+        copies[-1].start()
+    clipped = CLIP / jnp.maximum(hmax_ref[...], CLIP)
+    down = jnp.transpose(jnp.broadcast_to(clipped, (ROWS, ROWS)))
+    group = lax.div(lax.broadcasted_iota(jnp.int32, (ROWS, ROWS), 0), GROUP)
+    col = lax.broadcasted_iota(jnp.int32, (ROWS, ROWS), 1)
     big = jnp.full((ROWS, ROWS), jnp.inf, F32)
     per_query = jnp.min(jnp.where(group == lax.div(col, GROUP), down, big), axis=0, keepdims=True)
     per_key = jnp.min(
         jnp.where(group == jnp.minimum(col, KV_HEADS - 1), down, big), axis=0, keepdims=True
     )
-    fac_ref[0:1, :] = clipped / jnp.sqrt(per_query)
-    fac_ref[1:2, :] = jnp.sqrt(per_key)
-
-    for copies in (stage_a, stage_b, stage_c):
-        for c in copies:
-            c.wait_send()
-    for cond, make in flows.values():
-        @pl.when(cond)
-        def _():
-            for i in (K, V):
-                for h in range(CHUNKS):
-                    make(i, h).wait_send()
+    query_ref[...] = (clipped / jnp.sqrt(per_query))[:, :QUERY_HEADS]
+    key_ref[...] = jnp.sqrt(per_key)[:, :KV_HEADS]
+    for c in copies:
+        c.wait()
 
 
 def local(queries, keys, values, segments):
@@ -337,12 +372,12 @@
     hbm_spec = pl.BlockSpec(memory_space=pltpu.HBM)
     vmem_spec = pl.BlockSpec(memory_space=pltpu.VMEM)
     dma = pltpu.SemaphoreType.DMA
-    attended, factors = pl.pallas_call(
+    mixed, head_max = pl.pallas_call(
         kernel,
         name="packed_attention",
         out_shape=(
             jax.ShapeDtypeStruct((ROWS, width), BF16),
-            jax.ShapeDtypeStruct((2, ROWS), F32),
+            jax.ShapeDtypeStruct((1, ROWS), F32),
         ),
         in_specs=[hbm_spec, hbm_spec, hbm_spec, hbm_spec],
         out_specs=(vmem_spec, vmem_spec),
@@ -352,7 +387,6 @@
             pltpu.VMEM((4 * ROWS, kv_width), BF16),
             pltpu.VMEM((2, ROWS, kv_width), BF16),
             pltpu.VMEM((4, ROWS, ROWS), F32),
-            pltpu.VMEM((KV_HEADS, 4, GROUP * ROWS, ROWS), F32),
             pltpu.VMEM((KV_HEADS, GROUP * ROWS, ROWS), F32),
             pltpu.VMEM((KV_HEADS, GROUP * ROWS, 4 * ROWS), BF16),
             pltpu.VMEM(segments.shape, jnp.int32),
@@ -374,7 +408,21 @@
             collective_id=0, has_side_effects=True, vmem_limit_bytes=48 * 1024 * 1024
         ),
     )(*(pltpu.with_memory_space_constraint(a, pltpu.HBM) for a in (queries[0], keys[0], values[0], segments)))
-    return attended[None], factors[0, :QUERY_HEADS], factors[1, :KV_HEADS]
+    any_spec = pl.BlockSpec(memory_space=pl.ANY)
+    attended, query_factor, key_head_factor = pl.pallas_call(
+        finish,
+        name="finish",
+        out_shape=(
+            jax.ShapeDtypeStruct((ROWS, width), BF16),
+            jax.ShapeDtypeStruct((1, QUERY_HEADS), F32),
+            jax.ShapeDtypeStruct((1, KV_HEADS), F32),
+        ),
+        in_specs=[any_spec, vmem_spec],
+        out_specs=(any_spec, vmem_spec, vmem_spec),
+        scratch_shapes=[dma((4,))],
+        compiler_params=pltpu.CompilerParams(vmem_limit_bytes=8 * 1024 * 1024),
+    )(mixed, head_max)
+    return attended[None], query_factor[0], key_head_factor[0]
 
 
 def solution(mesh):

time: 62.8 us -> 57 us (0.908)
  Pallas kernels: 59.8 us -> 56.2 us
  local copies, waits for them, and re-layouts: 2.17 us -> 0 us
    pallas_call x1, Pallas kernels: 59.8 us -> 54.5 us  [local(): pl.pallas_call(kernel, name='packed_attention', out_shape=(jax.ShapeDtype...]
    pallas_call x0 -> x1, Pallas kernels: none -> 1.68 us  [local(): pl.pallas_call(finish, name='finish', out_shape=(jax.ShapeDtypeStruct((RO...]
    unnamed x1 -> x0, local copies, waits for them, and re-layouts: 1.14 us -> none
    squeeze x2 -> x0, local copies, waits for them, and re-layouts: 1.02 us -> none  [local(): return (attended[None], factors[0, :QUERY_HEADS], factors[1, :KV_HEADS])]
where the time goes in v3:
time: 57 us; the launch traced here: 56.8 us
  Pallas kernels  56.2 us (99%)
  between operations  0.64 us (1%)
    pallas_call x1, Pallas kernels, local(): pl.pallas_call(kernel, name='packed_attention', out_shape=(jax.ShapeDtype...  54.5 us
    pallas_call x1, Pallas kernels, local(): pl.pallas_call(finish, name='finish', out_shape=(jax.ShapeDtypeStruct((RO...  1.68 us

profile of v3, /device:TPU:3, one launch (start us, length us, event | category | flops | bytes accessed | tf_op | source)
XLA Modules:
  0.0 56.8 jit_solution(15198482667377207732)
XLA Ops:
  0.6 54.5 %packed_attention.1 = (bf16[128,6144]{1,0:T(8,128)(2,1)S(1)}, f32[1,128]{1,0:T(1,128)S(1)}) custom-call(bf16[128,6144]{1,0:T(8,128)(2,1)} %bitcast.6, bf16[128,768]{1,0:T(8,128)(2,1)} %bitcast.7, bf16[128,768]{1,0:T(8,128)(2,1)} %bitcast.8, s32[1,3072]{1,0:T(1,128)} %seg_hbm.1), custom_call_target="tpu_custom_call" | custom-call | tf_op jit(solution)/shard_map/packed_attention/pallas_call | solution.py:375
  55.1 1.7 %finish.1 = (bf16[128,6144]{1,0:T(8,128)(2,1)}, f32[1,48]{1,0:T(1,128)}, f32[1,6]{1,0:T(1,128)}) custom-call(bf16[128,6144]{1,0:T(8,128)(2,1)S(1)} %get-tuple-element.8.o_ref, f32[1,128]{1,0:T(1,128)S(1)} %get-tuple-element.9.hmax_ref), custom_call_target="tpu_custom_call" | custom-call | tf_op jit(solution)/shard_map/finish/pallas_call | solution.py:412

commit v4 on v3

--- a/solution.py
+++ b/solution.py
@@ -215,11 +215,11 @@
         start("cross_5", i)
         start("cross_6", i)
 
-    def take_relay(i):
+    def take_relay(i, also):
         for name in ("relay_6", "relay_1"):
             cond, make = flows[name]
             for h in chunks_of[name]:
-                @pl.when(cond)
+                @pl.when(cond & also)
                 def _():
                     await_part(RB, i, h)
                     make(i, h).start()
@@ -229,7 +229,7 @@
     start("f1", K)
     start("f2", V, also=x == 0)
     start("f1", V, also=x == 0)
-    take_relay(K)
+    take_relay(K, zh >= 0)
 
     def take_two(i):
         for h in range(CHUNKS):
@@ -280,7 +280,6 @@
     ar_a[0] = jnp.max(jnp.transpose(hm_ref[...]), axis=0, keepdims=True) * SCALE
     for c in stage_a:
         c.start()
-    take_relay(V)
 
     def p_body(c, carry):
         m = jnp.max(rm_ref[c], axis=1, keepdims=True).reshape(GROUP, ROWS, 1)
@@ -293,7 +292,11 @@
                 p_ref[c, :, t * ROWS : (t + 1) * ROWS] = p.astype(BF16).reshape(GROUP * ROWS, ROWS)
         return carry
 
-    lax.fori_loop(0, KV_HEADS, p_body, 0)
+    late = (s >= 8) & (r8 <= 2)
+    half = KV_HEADS // 2
+    take_relay(V, late)
+    lax.fori_loop(0, half, p_body, 0)
+    take_relay(V, jnp.logical_not(late))
 
     def finish_values():
         take(R1, V)
@@ -308,11 +311,13 @@
                 h = c * GROUP + g
                 o_ref[:, h * HEAD : (h + 1) * HEAD] = o[g * ROWS : (g + 1) * ROWS]
 
-    late = (s >= 8) & (r8 <= 2)
-
     @pl.when(jnp.logical_not(late))
     def _():
+        lax.fori_loop(half, KV_HEADS, p_body, 0)
         take_two(V)
+
+    @pl.when(x >= 2)
+    def _():
         finish_values()
 
     ar_b[0] = ar_finish(ar_a, stage_a)
@@ -321,13 +326,14 @@
 
     @pl.when(late)
     def _():
+        lax.fori_loop(half, KV_HEADS, p_body, 0)
         take_two(V)
 
     ar_c[0] = ar_finish(ar_b, stage_b)
     for c in stage_c:
         c.start()
 
-    @pl.when(late)
+    @pl.when(x <= 1)
     def _():
         finish_values()
 

time: 57 us -> 55.2 us (0.968)
  the two profiles are of different devices: /device:TPU:3 before, /device:TPU:2 now
where the time goes in v4:
time: 55.2 us; the launch traced here: 55.1 us
  Pallas kernels  54.4 us (99%)
  between operations  0.64 us (1%)
    pallas_call x1, Pallas kernels, local(): pl.pallas_call(kernel, name='packed_attention', out_shape=(jax.ShapeDtype...  52.7 us
    pallas_call x1, Pallas kernels, local(): pl.pallas_call(finish, name='finish', out_shape=(jax.ShapeDtypeStruct((RO...  1.68 us

profile of v4, /device:TPU:2, one launch (start us, length us, event | category | flops | bytes accessed | tf_op | source)
XLA Modules:
  0.0 55.1 jit_solution(17896431851843108000)
XLA Ops:
  0.6 52.7 %packed_attention.1 = (bf16[128,6144]{1,0:T(8,128)(2,1)S(1)}, f32[1,128]{1,0:T(1,128)S(1)}) custom-call(bf16[128,6144]{1,0:T(8,128)(2,1)} %bitcast.6, bf16[128,768]{1,0:T(8,128)(2,1)} %bitcast.7, bf16[128,768]{1,0:T(8,128)(2,1)} %bitcast.8, s32[1,3072]{1,0:T(1,128)} %seg_hbm.1), custom_call_target="tpu_custom_call" | custom-call | tf_op jit(solution)/shard_map/packed_attention/pallas_call | solution.py:381
  53.4 1.7 %finish.1 = (bf16[128,6144]{1,0:T(8,128)(2,1)}, f32[1,48]{1,0:T(1,128)}, f32[1,6]{1,0:T(1,128)}) custom-call(bf16[128,6144]{1,0:T(8,128)(2,1)S(1)} %get-tuple-element.8.o_ref, f32[1,128]{1,0:T(1,128)S(1)} %get-tuple-element.9.hmax_ref), custom_call_target="tpu_custom_call" | custom-call | tf_op jit(solution)/shard_map/finish/pallas_call | solution.py:418

commit v5 on v4

--- a/solution.py
+++ b/solution.py
@@ -23,6 +23,10 @@
 
 F1, F2, F34, F5, CROSS, RELAY = range(6)
 R1, R2, R3, RB = range(4)
+
+
+def far_first(n):
+    return sorted(range(1, n), key=lambda k: abs(2 * k - n))
 
 
 def kernel(
@@ -53,14 +57,14 @@
     load_seg = pltpu.make_async_copy(seg_hbm, seg_ref, load_sem.at[3])
     load_seg.start()
     barrier = pltpu.get_barrier_semaphore()
-    for n, dev in ((8, dev_a), (8, dev_b), (12, dev_c)):
-        for k in range(1, n):
-            pl.semaphore_signal(barrier, inc=1, device_id=dev(k), device_id_type=MESH)
-
     @pl.when((x == 0) & (zh >= 1))
     def _():
         for back in (jnp.where(core == 0, 3, 2), 6):
             pl.semaphore_signal(barrier, inc=1, device_id=(dp, s - back), device_id_type=MESH)
+
+    for n, dev in ((12, dev_c), (8, dev_b), (8, dev_a)):
+        for k in far_first(n):
+            pl.semaphore_signal(barrier, inc=1, device_id=dev(k), device_id_type=MESH)
 
     load_k = pltpu.make_async_copy(k_hbm, kall.at[pl.ds(3 * ROWS, ROWS)], load_sem.at[0])
     load_q = pltpu.make_async_copy(q_hbm, q_ref, load_sem.at[1])
@@ -265,7 +269,7 @@
                 device_id=dev(k),
                 device_id_type=MESH,
             )
-            for k in range(1, n)
+            for k in far_first(n)
         ]
 
     def ar_finish(buf, copies):

time: 55.2 us -> 55.1 us (level)
  no operation moved by 1% of the time
where the time goes in v5:
time: 55.1 us; the launch traced here: 54.9 us
  Pallas kernels  54.3 us (99%)
  between operations  0.64 us (1%)
    pallas_call x1, Pallas kernels, local(): pl.pallas_call(kernel, name='packed_attention', out_shape=(jax.ShapeDtype...  52.6 us
    pallas_call x1, Pallas kernels, local(): pl.pallas_call(finish, name='finish', out_shape=(jax.ShapeDtypeStruct((RO...  1.68 us

profile of v5, /device:TPU:2, one launch (start us, length us, event | category | flops | bytes accessed | tf_op | source)
XLA Modules:
  0.0 54.9 jit_solution(12453987238257243194)
XLA Ops:
  0.6 52.6 %packed_attention.1 = (bf16[128,6144]{1,0:T(8,128)(2,1)S(1)}, f32[1,128]{1,0:T(1,128)S(1)}) custom-call(bf16[128,6144]{1,0:T(8,128)(2,1)} %bitcast.6, bf16[128,768]{1,0:T(8,128)(2,1)} %bitcast.7, bf16[128,768]{1,0:T(8,128)(2,1)} %bitcast.8, s32[1,3072]{1,0:T(1,128)} %seg_hbm.1), custom_call_target="tpu_custom_call" | custom-call | tf_op jit(solution)/shard_map/packed_attention/pallas_call | solution.py:385
  53.3 1.7 %finish.1 = (bf16[128,6144]{1,0:T(8,128)(2,1)}, f32[1,48]{1,0:T(1,128)}, f32[1,6]{1,0:T(1,128)}) custom-call(bf16[128,6144]{1,0:T(8,128)(2,1)S(1)} %get-tuple-element.8.o_ref, f32[1,128]{1,0:T(1,128)S(1)} %get-tuple-element.9.hmax_ref), custom_call_target="tpu_custom_call" | custom-call | tf_op jit(solution)/shard_map/finish/pallas_call | solution.py:422
